TPU v7x, 32 devices: a whole 2x2x4 slice. The times are simulated.
32 devices in a mesh: dp: 8 (over z, y), rep: 4 (over x, core).
Axes of the slice: x: 2, y: 2, z: 4, core: 2. Of those that a mesh axis runs over, the one named last changes fastest.
Arguments:
- cell_input: bfloat16 [16384, 1024], P(('dp', 'rep')), may hold values from -6 to 6
- cotangent: bfloat16 [16384, 1024], P(('dp', 'rep')), may hold values from -6 to 6
- segment_ids: int32 [32, 512], P(('dp', 'rep')), may hold values from 0 to 15, never falling along the last dimension, each value on 1 to 128 neighbouring positions
- lengths: int32 [32], P(('dp', 'rep')), may hold values from 256 to 512
- w_qkv: bfloat16 [1024, 3072], P('dp'), may hold values from -0.1875 to 0.1875
- query_bias: bfloat16 [1024], P('dp'), may hold values from -1.75 to 1.75
- value_bias: bfloat16 [1024], P('dp'), may hold values from -1.75 to 1.75
- w_out: bfloat16 [1024, 1024], P('dp'), may hold values from -1 to 1
- out_bias: bfloat16 [1024], P('dp'), may hold values from -1.75 to 1.75
- w_up: bfloat16 [1024, 4096], P('dp'), may hold values from -0.1875 to 0.1875
- up_bias: bfloat16 [4096], P('dp'), may hold values from -1.75 to 1.75
- w_down: bfloat16 [4096, 1024], P('dp'), may hold values from -0.09375 to 0.09375
- down_bias: bfloat16 [1024], P('dp'), may hold values from -1.75 to 1.75
- norm1_gain: bfloat16 [1024], P('dp'), may hold values from 0.5 to 1.5
- norm1_bias: bfloat16 [1024], P('dp'), may hold values from -1.75 to 1.75
- norm2_gain: bfloat16 [1024], P('dp'), may hold values from 0.5 to 1.5
- norm2_bias: bfloat16 [1024], P('dp'), may hold values from -1.75 to 1.75
Outputs:
- block_out: bfloat16 [16384, 1024], P(('dp', 'rep'))
- input_grad: bfloat16 [16384, 1024], P(('dp', 'rep'))
- grad_qkv: float32 [1024, 3072], P('dp')
- grad_query_bias: float32 [1024], P('dp')
- grad_value_bias: float32 [1024], P('dp')
- grad_out: float32 [1024, 1024], P('dp')
- grad_out_bias: float32 [1024], P('dp')
- grad_up: float32 [1024, 4096], P('dp')
- grad_up_bias: float32 [4096], P('dp')
- grad_down: float32 [4096, 1024], P('dp')
- grad_down_bias: float32 [1024], P('dp')
- grad_norm1_gain: float32 [1024], P('dp')
- grad_norm1_bias: float32 [1024], P('dp')
- grad_norm2_gain: float32 [1024], P('dp')
- grad_norm2_bias: float32 [1024], P('dp')
Inputs may be any that keep to these rules, and one draw needn't show every extreme that they name: `segment_ids`: in each sequence the ids never fall; each of the 16 slides holds 1 to 128 cells, and one holds exactly 128. `lengths`: rows of a sequence at or past its length are padding.
All inputs are finite; a program needn't handle non-finite values.
Results may differ from a plain program's by a relative error of at most 0.015.
Values may be sent and summed in bfloat16 or wider, within the bound.
No kernel may reach another device: no remote copies, remote signals or barrier semaphores. Data moves between devices by JAX's collectives and lax.ppermute only.
A program may use at most 192 MiB of HBM per device.

v0:
```python
import math
import jax
import jax.numpy as jnp
from jax import lax
from jax.sharding import PartitionSpec as P

HEAD_DIM = 64


def normalize(values_in):
    row_mean = jnp.mean(values_in, axis=-1, keepdims=True)
    centred = values_in - row_mean
    inv_std = lax.rsqrt(jnp.mean(centred * centred, axis=-1, keepdims=True) + 1e-05)
    return (centred * inv_std, inv_std)


def norm_back(incoming, normed, inv_std, gain_vec):
    scaled = incoming * gain_vec
    return inv_std * (
        scaled
        - jnp.mean(scaled, axis=-1, keepdims=True)
        - normed * jnp.mean(scaled * normed, axis=-1, keepdims=True)
    )


def positions(length, model_width):
    places = jnp.arange(length, dtype=jnp.float32)[:, None]
    frequency = jnp.exp(
        jnp.arange(model_width // 2, dtype=jnp.float32) * (-2.0 * math.log(10000.0) / model_width)
    )
    angles = places * frequency[None, :]
    return jnp.stack([jnp.sin(angles), jnp.cos(angles)], axis=-1).reshape(length, model_width)


def gelu_slope(values_in):
    normal_cdf = 0.5 * (1.0 + lax.erf(values_in * (1.0 / math.sqrt(2.0))))
    return normal_cdf + values_in * jnp.exp(-0.5 * values_in * values_in) * (
        1.0 / math.sqrt(2.0 * math.pi)
    )


def block_mask(begin_row, block_rows, seg_row, live_cells):
    places = jnp.arange(seg_row.shape[0], dtype=jnp.int32)
    rows_at = begin_row + jnp.arange(block_rows, dtype=jnp.int32)
    return (seg_row[:, None] == seg_row[None, :]) & live_cells[:, None] & live_cells[None, :] | (
        rows_at[:, None] == places[None, :]
    )


def masked_scores(block_q, key_vecs, begin_row, block_rows, seg_row, live_cells):
    score_scale = 1.0 / math.sqrt(HEAD_DIM)
    scores = (
        jnp.einsum("qhd,khd->hqk", block_q, key_vecs, preferred_element_type=jnp.float32)
        * score_scale
    )
    return jnp.where(block_mask(begin_row, block_rows, seg_row, live_cells)[None], scores, -1e30)


def attention_forward(queries, key_vecs, values, seg_row, live_cells, block_rows):
    begin_rows = jnp.arange(queries.shape[0] // block_rows, dtype=jnp.int32) * block_rows

    def query_block(begin_row):
        scores = masked_scores(queries, key_vecs, begin_row, block_rows, seg_row, live_cells)
        row_max = jnp.max(scores, axis=-1, keepdims=True)
        exp_scores = jnp.exp(scores - row_max)
        row_total = jnp.sum(exp_scores, axis=-1, keepdims=True)
        weights = (exp_scores / row_total).astype(jnp.bfloat16)
        attended = jnp.einsum("hqk,khd->qhd", weights, values, preferred_element_type=jnp.float32)
        return (attended.astype(jnp.bfloat16), (row_max + jnp.log(row_total))[..., 0])

    attended, log_totals = lax.map(query_block, begin_rows)
    return (attended.reshape(queries.shape), log_totals)


def attention_backward(
    queries, key_vecs, values, attended_grad, log_totals, seg_row, live_cells, block_rows
):
    score_scale = 1.0 / math.sqrt(HEAD_DIM)
    begin_rows = jnp.arange(queries.shape[0] // block_rows, dtype=jnp.int32) * block_rows

    def query_block(running, inputs):
        begin_row, block_log = inputs
        key_total, value_total = running
        scores = masked_scores(queries, key_vecs, begin_row, block_rows, seg_row, live_cells)
        weights_f = jnp.exp(scores - block_log[..., None])
        value_total = value_total + jnp.einsum(
            "hqk,qhd->khd",
            weights_f.astype(jnp.bfloat16),
            attended_grad,
            preferred_element_type=jnp.float32,
        )
        prob_grad = jnp.einsum(
            "qhd,khd->hqk", attended_grad, values, preferred_element_type=jnp.float32
        )
        dscore = (
            weights_f * (prob_grad - jnp.sum(prob_grad * weights_f, axis=-1, keepdims=True))
        ).astype(jnp.bfloat16)
        block_dq = (
            jnp.einsum("hqk,khd->qhd", dscore, key_vecs, preferred_element_type=jnp.float32)
            * score_scale
        ).astype(jnp.bfloat16)
        key_total = (
            key_total
            + jnp.einsum("hqk,qhd->khd", dscore, queries, preferred_element_type=jnp.float32)
            * score_scale
        )
        return ((key_total, value_total), block_dq)

    zero_acc = jnp.zeros(queries.shape, jnp.float32)
    (key_total, value_total), query_grad = lax.scan(
        query_block, (zero_acc, zero_acc), (begin_rows, log_totals)
    )
    return (
        query_grad.reshape(queries.shape),
        key_total.astype(jnp.bfloat16),
        value_total.astype(jnp.bfloat16),
    )


def forward_pass(gathered, cell_input, pos_table, seg_row, live_cells, block_rows):
    (
        w_qkv,
        query_bias,
        value_bias,
        w_out,
        out_bias,
        w_up,
        up_bias,
        w_down,
        down_bias,
        norm1_gain,
        norm1_bias,
        norm2_gain,
        norm2_bias,
    ) = gathered
    length, model_width = cell_input.shape
    head_count = model_width // HEAD_DIM
    cells_f = cell_input.astype(jnp.float32)
    normed_one, inv_one = normalize(cells_f)
    normed_in = (
        normed_one * norm1_gain.astype(jnp.float32) + norm1_bias.astype(jnp.float32) + pos_table
    ).astype(jnp.bfloat16)
    projected = jnp.dot(normed_in, w_qkv, preferred_element_type=jnp.float32)
    queries = (
        (projected[:, :model_width] + query_bias.astype(jnp.float32))
        .astype(jnp.bfloat16)
        .reshape(length, head_count, HEAD_DIM)
    )
    key_vecs = (
        projected[:, model_width : 2 * model_width]
        .astype(jnp.bfloat16)
        .reshape(length, head_count, HEAD_DIM)
    )
    values = (
        (projected[:, 2 * model_width :] + value_bias.astype(jnp.float32))
        .astype(jnp.bfloat16)
        .reshape(length, head_count, HEAD_DIM)
    )
    attended, log_totals = attention_forward(
        queries, key_vecs, values, seg_row, live_cells, block_rows
    )
    attended = attended.reshape(length, model_width)
    middle = (
        cells_f
        + jnp.dot(attended, w_out, preferred_element_type=jnp.float32)
        + out_bias.astype(jnp.float32)
    )
    normed_two, inv_two = normalize(middle)
    hidden_in = (
        normed_two * norm2_gain.astype(jnp.float32) + norm2_bias.astype(jnp.float32)
    ).astype(jnp.bfloat16)
    pre_act = jnp.dot(hidden_in, w_up, preferred_element_type=jnp.float32) + up_bias.astype(
        jnp.float32
    )
    hidden = jax.nn.gelu(pre_act, approximate=False).astype(jnp.bfloat16)
    result = (
        middle
        + jnp.dot(hidden, w_down, preferred_element_type=jnp.float32)
        + down_bias.astype(jnp.float32)
    )
    kept = (
        normed_in,
        normed_one,
        inv_one,
        queries,
        key_vecs,
        values,
        attended,
        log_totals,
        normed_two,
        inv_two,
        hidden_in,
        pre_act,
        hidden,
    )
    return (result.astype(jnp.bfloat16), kept)


def backward_pass(gathered, kept, cotangent, seg_row, live_cells, block_rows):
    (
        w_qkv,
        query_bias,
        value_bias,
        w_out,
        out_bias,
        w_up,
        up_bias,
        w_down,
        down_bias,
        norm1_gain,
        norm1_bias,
        norm2_gain,
        norm2_bias,
    ) = gathered
    (
        normed_in,
        normed_one,
        inv_one,
        queries,
        key_vecs,
        values,
        attended,
        log_totals,
        normed_two,
        inv_two,
        hidden_in,
        pre_act,
        hidden,
    ) = kept
    length = attended.shape[0]
    upstream = cotangent.astype(jnp.float32)
    grad_down = jnp.einsum("tf,td->fd", hidden, cotangent, preferred_element_type=jnp.float32)
    grad_down_bias = jnp.sum(upstream, axis=0)
    hidden_grad = jnp.einsum("td,fd->tf", cotangent, w_down, preferred_element_type=jnp.float32)
    pre_grad = (hidden_grad * gelu_slope(pre_act)).astype(jnp.bfloat16)
    grad_up = jnp.einsum("td,tf->df", hidden_in, pre_grad, preferred_element_type=jnp.float32)
    grad_up_bias = jnp.sum(pre_grad.astype(jnp.float32), axis=0)
    mid_grad = jnp.einsum("tf,df->td", pre_grad, w_up, preferred_element_type=jnp.float32)
    grad_gain_two = jnp.sum(mid_grad * normed_two, axis=0)
    grad_shift_two = jnp.sum(mid_grad, axis=0)
    middle_grad = upstream + norm_back(
        mid_grad, normed_two, inv_two, norm2_gain.astype(jnp.float32)
    )
    branch_grad = middle_grad.astype(jnp.bfloat16)
    grad_out = jnp.einsum("td,te->de", attended, branch_grad, preferred_element_type=jnp.float32)
    grad_out_bias = jnp.sum(branch_grad.astype(jnp.float32), axis=0)
    attended_grad = jnp.einsum(
        "te,de->td", branch_grad, w_out, preferred_element_type=jnp.float32
    ).astype(jnp.bfloat16)
    query_grad, key_grad, value_grad = attention_backward(
        queries,
        key_vecs,
        values,
        attended_grad.reshape(queries.shape),
        log_totals,
        seg_row,
        live_cells,
        block_rows,
    )
    query_grad = query_grad.reshape(length, -1)
    value_grad = value_grad.reshape(length, -1)
    proj_grad = jnp.concatenate([query_grad, key_grad.reshape(length, -1), value_grad], axis=1)
    grad_qkv = jnp.einsum("td,te->de", normed_in, proj_grad, preferred_element_type=jnp.float32)
    grad_query_bias = jnp.sum(query_grad.astype(jnp.float32), axis=0)
    grad_value_bias = jnp.sum(value_grad.astype(jnp.float32), axis=0)
    in_grad = jnp.einsum("te,de->td", proj_grad, w_qkv, preferred_element_type=jnp.float32)
    grad_gain_one = jnp.sum(in_grad * normed_one, axis=0)
    grad_shift_one = jnp.sum(in_grad, axis=0)
    input_grad = (
        middle_grad + norm_back(in_grad, normed_one, inv_one, norm1_gain.astype(jnp.float32))
    ).astype(jnp.bfloat16)
    grads = (
        grad_qkv,
        grad_query_bias,
        grad_value_bias,
        grad_out,
        grad_out_bias,
        grad_up,
        grad_up_bias,
        grad_down,
        grad_down_bias,
        grad_gain_one,
        grad_shift_one,
        grad_gain_two,
        grad_shift_two,
    )
    return (input_grad, grads)


VECTORS = (1, 2, 4, 6, 8, 9, 10, 11, 12)
MATRICES = (0, 3, 5, 7)
EVERY = ("dp", "rep")


def gather_matrix(shard):
    part_rows = shard.shape[0] // lax.axis_size("rep")
    own = lax.dynamic_slice_in_dim(shard, lax.axis_index("rep") * part_rows, part_rows, 0)
    return lax.all_gather(own, EVERY, axis=0, tiled=True)


def gather_vectors(shards):
    packed = jnp.concatenate(shards)
    whole = lax.all_gather(packed, "dp", axis=0, tiled=False)
    vectors, begin = ([], 0)
    for shard in shards:
        vectors.append(whole[:, begin : begin + shard.shape[0]].reshape(-1))
        begin += shard.shape[0]
    return vectors


def reduce_matrix(grad):
    part = lax.psum_scatter(grad.astype(jnp.bfloat16), EVERY, scatter_dimension=0, tiled=True)
    return lax.all_gather(part, "rep", axis=0, tiled=True).astype(jnp.float32)


def reduce_vectors(grads):
    owners = lax.axis_size("dp")
    packed = jnp.concatenate([grad.reshape(owners, -1) for grad in grads], axis=1)
    total = lax.psum(packed, EVERY)
    own = lax.dynamic_index_in_dim(total, lax.axis_index("dp"), 0, keepdims=False)
    outs, begin = ([], 0)
    for grad in grads:
        size = grad.shape[0] // owners
        outs.append(own[begin : begin + size])
        begin += size
    return outs


def on_device(cell_input, cotangent, segment_ids, lengths, *shards):
    gathered = [None] * len(shards)
    for place, vector in zip(VECTORS, gather_vectors([shards[place] for place in VECTORS])):
        gathered[place] = vector
    for place in MATRICES:
        gathered[place] = gather_matrix(shards[place])
    length, model_width = cell_input.shape
    block_rows = min(length, 512)
    seg_row = segment_ids[0]
    live_cells = jnp.arange(length, dtype=jnp.int32) < lengths[0]
    pos_table = positions(length, model_width)
    block_out, kept = forward_pass(gathered, cell_input, pos_table, seg_row, live_cells, block_rows)
    input_grad, grads = backward_pass(gathered, kept, cotangent, seg_row, live_cells, block_rows)
    summed = [None] * len(grads)
    for place in (7, 5, 3, 0):
        summed[place] = reduce_matrix(grads[place])
    for place, vector in zip(VECTORS, reduce_vectors([grads[place] for place in VECTORS])):
        summed[place] = vector
    return (block_out, input_grad) + tuple(summed)


def solution(mesh):
    in_specs = (
        P(("dp", "rep"), None),
        P(("dp", "rep"), None),
        P(("dp", "rep"), None),
        P(("dp", "rep")),
        P("dp", None),
        P("dp"),
        P("dp"),
        P("dp", None),
        P("dp"),
        P("dp", None),
        P("dp"),
        P("dp", None),
        P("dp"),
        P("dp"),
        P("dp"),
        P("dp"),
        P("dp"),
    )
    out_specs = (
        P(("dp", "rep"), None),
        P(("dp", "rep"), None),
        P("dp", None),
        P("dp"),
        P("dp"),
        P("dp", None),
        P("dp"),
        P("dp", None),
        P("dp"),
        P("dp", None),
        P("dp"),
        P("dp"),
        P("dp"),
        P("dp"),
        P("dp"),
    )
    return jax.shard_map(
        on_device, mesh=mesh, in_specs=in_specs, out_specs=out_specs, check_vma=False
    )
```

profile of v0, /device:TPU:0, one launch (start us, length us, event | category | flops | bytes accessed | tf_op | source)
XLA Modules:
  0.0 915.2 jit_solution(13305810542900627797)
XLA Ops:
  7.2 1.7 constant_dynamic-slice_fusion.4
  9.0 1.5 constant_dynamic-slice_fusion.3
  11.4 1.7 constant_dynamic-slice_fusion.1
  13.8 0.9 dynamic-update-slice.9
  14.7 0.8 dynamic-update-slice.10
  15.5 0.8 dynamic-update-slice.11
  16.3 0.9 dynamic-update-slice.12
  17.2 0.8 dynamic-update-slice.13
  18.0 0.8 dynamic-update-slice.14
  18.9 0.8 dynamic-update-slice.15
  21.3 32.7 %all-gather.1 = bf16[8,1,1536]{2,1,0:T(2,128)(2,1)S(1)} all-gather(bf16[1,1,1536]{2,1,0:T(2,128)(2,1)S(1)} %reshape.394), channel_id=2, replica_groups=mesh['dp'=8,'rep'=4] {'dp'}, dimensions={0}, use_global_device_ids=true | all-gather | bytes 27648 | tf_op jit(solution)/shard_map/all_gather | solution.py:303
  54.0 3.7 fusion.47
  58.0 2.6 copy.62
  60.6 3.7 reshape.368
  64.3 1.9 copy.63
  67.8 1.5 fusion.30
  69.3 14.1 %all-gather.9.cloned.1.call-done = bf16[1024,3072]{1,0:T(8,128)(2,1)} async-done(((bf16[32,3072]{1,0:T(8,128)(2,1)}), bf16[1024,3072]{1,0:T(8,128)(2,1)}) %all-gather.9.cloned.1.call-update) | async-done | bytes 6291472 | tf_op jit(solution)/shard_map/all_gather | solution.py:298
  83.4 5.8 fusion.65
  89.2 1.1 slice.165
  90.4 1.6 fusion.39
  92.5 1.9 copy.66
  94.4 2.7 copy.64
  97.1 7.4 fusion.63
  104.4 8.4 fusion
  112.9 8.9 fusion.41
  121.7 19.3 %all-gather.11.cloned.1.call-done = bf16[1024,1024]{1,0:T(8,128)(2,1)} async-done(((bf16[32,1024]{1,0:T(8,128)(2,1)}), bf16[1024,1024]{1,0:T(8,128)(2,1)}) %all-gather.11.cloned.1.call-update) | async-done | bytes 2097168 | tf_op jit(solution)/shard_map/all_gather | solution.py:298
  141.0 3.3 fusion.64
  144.7 75.7 %all-gather.13.cloned.1.call-done = bf16[1024,4096]{1,0:T(8,128)(2,1)} async-done(((bf16[32,4096]{1,0:T(8,128)(2,1)}), bf16[1024,4096]{1,0:T(8,128)(2,1)}) %all-gather.13.cloned.1.call-update) | async-done | bytes 8388624 | tf_op jit(solution)/shard_map/all_gather | solution.py:298
  220.4 27.0 %fusion.4 = (bf16[512,4096]{1,0:T(8,128)(2,1)}, f32[512,4096]{1,0:T(8,128)}) fusion(f32[4096]{0:T(1024)S(1)} %bitcast.148, bf16[1024,4096]{1,0:T(8,128)(2,1)} %all-gather.13.cloned.1.call-done, f32[512,1024]{1,0:T(8,128)S(1)} %get-tuple-element.106, f32[1024]{0:T(1024)S(1)} %get-tuple-element.94, f32[1024]{0:T(1024)S(1)} %get-tuple-element.95, ...), kind=kOutput, calls=%fused_computation.12 | convolution fusion | flops 4436000768 | bytes 23097344 | tf_op jit(solution)/shard_map/dot_general | solution.py:172
  247.4 51.4 %all-gather.15.cloned.1.call-done = bf16[4096,1024]{1,0:T(8,128)(2,1)} async-done(((bf16[128,1024]{1,0:T(8,128)(2,1)}), bf16[4096,1024]{1,0:T(8,128)(2,1)}) %all-gather.15.cloned.1.call-update) | async-done | bytes 8388624 | tf_op jit(solution)/shard_map/all_gather | solution.py:298
  298.8 11.3 %convert_reduce_fusion = (f32[4096]{0:T(1024)}, bf16[512,4096]{1,0:T(8,128)(2,1)S(1)}) fusion(f32[512,4096]{1,0:T(8,128)} %get-tuple-element.108, f32[4096]{0:T(1024)S(1)} %bitcast.149, bf16[4096,1024]{1,0:T(8,128)(2,1)} %all-gather.15.cloned.1.call-done, bf16[512,1024]{1,0:T(8,128)(2,1)S(1)} %copy-done.15), kind=kOutput, calls=%fused_computation.20 | convolution fusion | flops 4322226176 | bytes 22052864 | tf_op jit(solution)/shard_map/td,fd->tf/dot_general | solution.py:234
  310.1 2.0 copy-done.30
  312.1 7.3 convolution_convert_fusion.1
  319.5 9.1 convolution_convert_fusion
  329.3 9.4 %multiply_reduce_fusion.1 = (f32[1024]{0:T(1024)}, f32[512]{0:T(512)S(1)}, f32[512]{0:T(512)S(1)}, f32[1024]{0:T(1024)S(1)}, f32[512,1024]{1,0:T(8,128)S(1)}) fusion(f32[512,1024]{1,0:T(8,128)S(1)} %get-tuple-element.106, f32[512]{0:T(512)S(1)} %add_rsqrt_fusion, f32[512]{0:T(512)S(1)} %broadcast_multiply_fusion.4, f32[1024]{0:T(1024)S(1)} %get-tuple-element.95, ...), kind=kOutput, calls=%fused_computation.70 | convolution fusion | flops 4299682816 | bytes 16797696 | tf_op jit(solution)/shard_map/tf,df->td/dot_general | solution.py:238
  338.7 1.0 convert_reduce_fusion.3
  339.7 1.3 copy-done.12
  341.0 1.3 convolution_convert_fusion.4
  342.9 4.6 convolution_convert_fusion.3
  347.6 14.7 %multiply_reduce_fusion = (f32[16,512]{1,0:T(8,128)}, f32[16,512,512]{1,2,0:T(8,128)}) fusion(f32[16,512,512]{1,2,0:T(8,128)} %get-tuple-element.104, f32[16,512]{1,0:T(8,128)} %log_add_fusion, bf16[512,16,64]{0,2,1:T(8,128)(2,1)S(1)} %bitcast.134, bf16[512,16,64]{0,2,1:T(8,128)(2,1)} %bitcast.136), kind=kOutput, calls=%fused_computation.1 | convolution fusion | flops 549445632 | bytes 35717120 | tf_op jit(solution)/shard_map/while/body/eval_jaxpr/qhd,khd->hqk/dot_general | solution.py:92
  362.4 1.0 slice-done.2
  363.4 1.2 slice-done.3
  364.6 10.5 %multiply_convert_fusion = bf16[16,512,512]{1,2,0:T(8,128)(2,1)} fusion(f32[16,512,512]{1,2,0:T(8,128)} %get-tuple-element.111, f32[16,512,512]{1,2,0:T(8,128)S(1)} %bitcast.129, f32[16,512]{1,0:T(8,128)} %get-tuple-element.110, f32[16,512]{1,0:T(8,128)} %log_add_fusion), kind=kLoop, calls=%fused_computation | loop fusion | flops 16777216 | bytes 42008576 | tf_op jit(solution)/shard_map/while/body/eval_jaxpr/convert_element_type | solution.py:97
  375.2 6.6 multiply_convert_fusion.1
  381.8 1.5 convert_reduce_fusion.5
  383.3 8.9 convert_reduce_fusion.4
  392.2 1.0 copy-done.17
  393.1 8.4 convolution_convert_fusion.2
  402.8 8.5 fusion.36
  411.3 57.1 %reduce-scatter.9.cloned.1.call-done = bf16[32,4096]{1,0:T(8,128)(2,1)} async-done(((bf16[1024,4096]{1,0:T(8,128)(2,1)}), bf16[32,4096]{1,0:T(8,128)(2,1)}) %reduce-scatter.9.cloned.1.call-update) | async-done | bytes 262160 | tf_op jit(solution)/shard_map/reduce_scatter | solution.py:312
  468.5 40.1 %psum.7 = f32[8,1536]{1,0:T(8,128)S(1)} all-reduce(f32[8,1536]{1,0:T(8,128)S(1)} %constant_dynamic-update-slice_fusion), channel_id=1, replica_groups=mesh['dp'=8,'rep'=4] {'dp','rep'}, use_global_device_ids=true, to_apply=%region_21.22 | all-reduce | flops 12288 | bytes 98304 | tf_op jit(solution)/shard_map/psum | solution.py:319
  509.9 3.9 fusion.35
  513.9 102.6 %reduce-scatter.11.cloned.1.call-done = bf16[128,1024]{1,0:T(8,128)(2,1)} async-done(((bf16[4096,1024]{1,0:T(8,128)(2,1)}), bf16[128,1024]{1,0:T(8,128)(2,1)}) %reduce-scatter.11.cloned.1.call-update) | async-done | bytes 262160 | tf_op jit(solution)/shard_map/reduce_scatter | solution.py:312
  616.6 10.2 %add_convert_fusion = bf16[512,1024]{1,0:T(8,128)(2,1)} fusion(f32[512,1024]{1,0:T(8,128)S(1)} %copy-done.6, bf16[512,4096]{1,0:T(8,128)(2,1)} %get-tuple-element.107, bf16[4096,1024]{1,0:T(8,128)(2,1)} %all-gather.15.cloned.1.call-done, f32[1024]{0:T(1024)S(1)} %copy-done.28), kind=kOutput, calls=%fused_computation.77 | convolution fusion | flops 4296540160 | bytes 15732736 | tf_op jit(solution)/shard_map/dot_general | solution.py:178
  626.8 126.4 %reduce-scatter.7.cloned.1.call-done = bf16[32,1024]{1,0:T(8,128)(2,1)} async-done(((bf16[1024,1024]{1,0:T(8,128)(2,1)}), bf16[32,1024]{1,0:T(8,128)(2,1)}) %reduce-scatter.7.cloned.1.call-update) | async-done | bytes 65552 | tf_op jit(solution)/shard_map/reduce_scatter | solution.py:312
  753.2 6.0 all_gather.37
  759.1 0.8 convert_element_type.253
  760.0 109.7 %reduce-scatter.5.cloned.1.call-done = bf16[32,3072]{1,0:T(8,128)(2,1)} async-done(((bf16[1024,3072]{1,0:T(8,128)(2,1)}), bf16[32,3072]{1,0:T(8,128)(2,1)}) %reduce-scatter.5.cloned.1.call-update) | async-done | bytes 196624 | tf_op jit(solution)/shard_map/reduce_scatter | solution.py:312
  869.7 8.8 all_gather.36
  878.5 1.3 convert_element_type.247
  879.8 7.2 all-gather.17.cloned.1.call-done
  887.0 2.8 convert_element_type.255
  889.7 15.4 %all-gather.19.cloned.1.call-done = bf16[512,1024]{1,0:T(8,128)(2,1)} async-done(((bf16[128,1024]{1,0:T(8,128)(2,1)}), bf16[512,1024]{1,0:T(8,128)(2,1)}) %all-gather.19.cloned.1.call-update) | async-done | bytes 1048592 | tf_op jit(solution)/shard_map/all_gather | solution.py:313
  905.1 2.8 convert_element_type.257
  (126 shorter events, 9.4 us)
Async XLA Ops:
  7.2 3.4 copy-start
  7.2 76.2 %all-gather.9.cloned.1.call-start = ((), (), s32[]{:S(2)}) async-start(), calls=%async_computation.4 | async-start | bytes 6488064 | tf_op jit(solution)/shard_map/all_gather | solution.py:298
  9.0 132.1 %all-gather.11.cloned.1.call-start = ((), (), s32[]{:S(2)}) async-start(), calls=%async_computation.5 | async-start | bytes 2162688 | tf_op jit(solution)/shard_map/all_gather | solution.py:298
  10.5 209.9 %all-gather.13.cloned.1.call-start = ((), (), s32[]{:S(2)}) async-start(), calls=%async_computation.6 | async-start | bytes 8650752 | tf_op jit(solution)/shard_map/all_gather | solution.py:298
  11.3 287.5 %all-gather.15.cloned.1.call-start = ((), (), s32[]{:S(2)}) async-start(), calls=%async_computation.7 | async-start | bytes 8650752 | tf_op jit(solution)/shard_map/all_gather | solution.py:298
  13.1 455.3 %reduce-scatter.9.cloned.1.call-start = ((), (), s32[]{:S(2)}) async-start(), calls=%async_computation.10 | async-start | bytes 8650752 | tf_op jit(solution)/shard_map/reduce_scatter | solution.py:312
  58.0 8.3 copy-start.3
  60.6 6.9 copy-start.27
  66.5 22.7 %copy-start.22 = (f32[512]{0:T(512)}, f32[512]{0:T(512)S(1)}, u32[]{:S(2)}) copy-start(f32[512]{0:T(512)S(1)} %broadcast_multiply_fusion.5) | copy-start | bytes 6148
  66.9 22.3 %copy-start.24 = (f32[512]{0:T(512)}, f32[512]{0:T(512)S(1)}, u32[]{:S(2)}) copy-start(f32[512]{0:T(512)S(1)} %add_rsqrt_fusion.1) | copy-start | bytes 6148
  67.5 21.7 %copy-start.20 = (f32[1024]{0:T(1024)}, f32[1024]{0:T(1024)S(1)}, u32[]{:S(2)}) copy-start(f32[1024]{0:T(1024)S(1)} %get-tuple-element.100) | copy-start | bytes 12292
  92.5 11.9 %copy-start.9 = (bf16[512,1024]{0,1:T(8,128)(2,1)}, bf16[512,1024]{0,1:T(8,128)(2,1)S(1)}, u32[]{:S(2)}) copy-start(bf16[512,1024]{0,1:T(8,128)(2,1)S(1)} %copy.65) | copy-start | bytes 3145732
  94.4 10.1 %copy-start.7 = (bf16[512,1024]{0,1:T(8,128)(2,1)}, bf16[512,1024]{0,1:T(8,128)(2,1)S(1)}, u32[]{:S(2)}) copy-start(bf16[512,1024]{0,1:T(8,128)(2,1)S(1)} %copy.66) | copy-start | bytes 3145732
  104.4 8.4 copy-start.13
  144.3 194.4 %copy-start.5 = (f32[512,1024]{1,0:T(8,128)}, f32[512,1024]{1,0:T(8,128)S(1)}, u32[]{:S(2)}) copy-start(f32[512,1024]{1,0:T(8,128)S(1)} %get-tuple-element.106) | copy-start | bytes 6291460
  220.4 78.4 %copy-start.15 = (bf16[512,1024]{1,0:T(8,128)(2,1)S(1)}, bf16[512,1024]{1,0:T(8,128)(2,1)}, u32[]{:S(2)}) copy-start(bf16[512,1024]{1,0:T(8,128)(2,1)} %param.18) | copy-start | bytes 3145732
  310.1 2.0 copy-start.30
  319.5 297.0 %reduce-scatter.11.cloned.1.call-start = ((), (), s32[]{:S(2)}) async-start(), calls=%async_computation.12 | async-start | bytes 8650752 | tf_op jit(solution)/shard_map/reduce_scatter | solution.py:312
  328.6 424.6 %reduce-scatter.7.cloned.1.call-start = ((), (), s32[]{:S(2)}) async-start(), calls=%async_computation.9 | async-start | bytes 2162688 | tf_op jit(solution)/shard_map/reduce_scatter | solution.py:312
  338.7 2.3 copy-start.14
  339.7 1.3 copy-start.12
  339.7 3.2 copy-start.18
  342.9 19.5 %copy-start.10 = (bf16[512,1024]{0,1:T(8,128)(2,1)}, bf16[512,1024]{0,1:T(8,128)(2,1)S(1)}, u32[]{:S(2)}) copy-start(bf16[512,1024]{0,1:T(8,128)(2,1)S(1)} %copy.68) | copy-start | bytes 3145732
  347.5 522.1 %reduce-scatter.5.cloned.1.call-start = ((), (), s32[]{:S(2)}) async-start(), calls=%async_computation.8 | async-start | bytes 6488064 | tf_op jit(solution)/shard_map/reduce_scatter | solution.py:312
  347.6 14.8 %slice-start = ((s8[16777216]{0:T(1024)(128)(4,1)}), s8[4194304]{0:T(1024)(128)(4,1)S(1)}, s32[]{:S(2)}) async-start(s8[16777216]{0:T(1024)(128)(4,1)} %bitcast.128), calls=%async_computation.14 | async-start | bytes 8388608
  347.6 14.8 %slice-start.1 = ((s8[16777216]{0:T(1024)(128)(4,1)}), s8[4194304]{0:T(1024)(128)(4,1)S(1)}, s32[]{:S(2)}) async-start(s8[16777216]{0:T(1024)(128)(4,1)} %bitcast.128), calls=%async_computation.15 | async-start | bytes 8388608
  347.6 15.8 %slice-start.2 = ((s8[16777216]{0:T(1024)(128)(4,1)}), s8[4194304]{0:T(1024)(128)(4,1)S(1)}, s32[]{:S(2)}) async-start(s8[16777216]{0:T(1024)(128)(4,1)} %bitcast.128), calls=%async_computation.16 | async-start | bytes 8388608
  347.6 17.0 %slice-start.3 = ((s8[16777216]{0:T(1024)(128)(4,1)}), s8[4194304]{0:T(1024)(128)(4,1)S(1)}, s32[]{:S(2)}) async-start(s8[16777216]{0:T(1024)(128)(4,1)} %bitcast.128), calls=%async_computation.17 | async-start | bytes 8388608
  375.2 6.6 copy-start.2
  375.2 6.6 copy-start.8
  381.8 1.5 copy-start.11
  381.8 1.5 copy-start.19
  383.3 9.9 %copy-start.16 = (bf16[512,1024]{1,0:T(8,128)(2,1)S(1)}, bf16[512,1024]{1,0:T(8,128)(2,1)}, u32[]{:S(2)}) copy-start(bf16[512,1024]{1,0:T(8,128)(2,1)} %fusion.30) | copy-start | bytes 3145732
  392.2 1.0 copy-start.17
  401.5 0.7 copy-start.26
  401.5 1.2 copy-start.4
  401.5 1.2 copy-start.21
  401.5 1.2 copy-start.23
  401.5 1.2 copy-start.25
  401.6 485.4 %all-gather.17.cloned.1.call-start = ((), (), s32[]{:S(2)}) async-start(), calls=%async_computation.11 | async-start | bytes 1310720 | tf_op jit(solution)/shard_map/all_gather | solution.py:313
  402.8 65.7 %copy-start.29 = (f32[1024]{0:T(1024)S(1)}, f32[1024]{0:T(1024)}, u32[]{:S(2)}) copy-start(f32[1024]{0:T(1024)} %get-tuple-element.61) | copy-start | bytes 12292
  411.3 205.3 %copy-start.6 = (f32[512,1024]{1,0:T(8,128)S(1)}, f32[512,1024]{1,0:T(8,128)}, u32[]{:S(2)}) copy-start(f32[512,1024]{1,0:T(8,128)} %copy-done.5) | copy-start | bytes 6291460
  411.3 205.3 %copy-start.28 = (f32[1024]{0:T(1024)S(1)}, f32[1024]{0:T(1024)}, u32[]{:S(2)}) copy-start(f32[1024]{0:T(1024)} %get-tuple-element.93) | copy-start | bytes 12292
  468.4 436.6 %all-gather.19.cloned.1.call-start = ((), (), s32[]{:S(2)}) async-start(), calls=%async_computation.13 | async-start | bytes 1310720 | tf_op jit(solution)/shard_map/all_gather | solution.py:313
  616.5 291.3 %copy-start.1 = (bf16[128,4096]{1,0:T(8,128)(2,1)S(1)}, bf16[128,4096]{1,0:T(8,128)(2,1)}, u32[]{:S(2)}) copy-start(bf16[128,4096]{1,0:T(8,128)(2,1)} %param.26) | copy-start | bytes 3145732
Sparse Core Ops, SparseCore 0:
  11.4 71.9 all-gather.8
  86.3 54.7 all-gather.10
  144.5 75.8 all-gather.12
  223.1 75.6 all-gather.14
  319.6 148.7 reduce-scatter.8
  470.6 145.8 reduce-scatter.10
  618.8 134.3 reduce-scatter.6
  758.8 110.8 reduce-scatter.4
  871.3 15.6 all-gather.16
  888.4 16.6 all-gather.18
where the time goes:
time: 921 us; the launch traced here: 915 us
  waiting for transfers between devices  579 us (63%)
  matrix products  154 us (17%)
  blocking collectives  87.5 us (10%)
  other arithmetic  41.1 us (4%)
  local copies, waits for them, and re-layouts  36.9 us (4%)
  between operations  15.8 us (2%)
    reduce_scatter x4, waiting for transfers between devices, reduce_matrix(): lax.psum_scatter(grad.astype(jnp.bfloat16), EVERY, scatter_dimension=0, t...  396 us
    all_gather x4, waiting for transfers between devices, gather_matrix(): return lax.all_gather(own, EVERY, axis=0, tiled=True)  161 us
    psum x1, blocking collectives, reduce_vectors(): total = lax.psum(packed, EVERY)  40.1 us
    all_gather x1, blocking collectives, gather_vectors(): whole = lax.all_gather(packed, 'dp', axis=0, tiled=False)  32.7 us
    dot_general x1, matrix products, forward_pass(): jnp.dot(hidden_in, w_up, preferred_element_type=jnp.float32)  27 us
    all_gather x2, waiting for transfers between devices, reduce_matrix(): return lax.all_gather(part, 'rep', axis=0, tiled=True).astype(jnp.float32)  22.6 us
  transfers between devices with their start and end apart: 10, of which 10 were waited for; matrix products, arithmetic and copies ran while one was open for 22% of the time, Pallas kernels for 0%

commit v1 on v0

--- a/solution.py
+++ b/solution.py
@@ -316,7 +316,7 @@
 def reduce_vectors(grads):
     owners = lax.axis_size("dp")
     packed = jnp.concatenate([grad.reshape(owners, -1) for grad in grads], axis=1)
-    total = lax.psum(packed, EVERY)
+    total = jnp.sum(lax.all_gather(packed, EVERY), axis=0)
     own = lax.dynamic_index_in_dim(total, lax.axis_index("dp"), 0, keepdims=False)
     outs, begin = ([], 0)
     for grad in grads:

time: 921 us -> 978 us (1.062)
  waiting for transfers between devices: 579 us -> 683 us
  blocking collectives: 87.5 us -> 47.4 us
    reduce_scatter x4, waiting for transfers between devices: 396 us -> 457 us  [reduce_matrix(): lax.psum_scatter(grad.astype(jnp.bfloat16), EVERY, scatter_dimension=0, t...]
    all_gather x0 -> x1, waiting for transfers between devices: none -> 42.1 us  [reduce_vectors(): total = jnp.sum(lax.all_gather(packed, EVERY), axis=0)]
    psum x1 -> x0, blocking collectives: 40.1 us -> none  [reduce_vectors(): total = lax.psum(packed, EVERY)]
  transfers between devices with their start and end apart: 10 -> 11, of which waited for: 10 -> 11; matrix products, arithmetic and copies ran while one was open for 22% -> 20% of each run, Pallas kernels for 0% -> 0%
where the time goes in v1:
time: 978 us; the launch traced here: 973 us
  waiting for transfers between devices  683 us (70%)
  matrix products  154 us (16%)
  blocking collectives  47.4 us (5%)
  other arithmetic  37.5 us (4%)
  local copies, waits for them, and re-layouts  34.9 us (4%)
  between operations  15.4 us (2%)
    reduce_scatter x4, waiting for transfers between devices, reduce_matrix(): lax.psum_scatter(grad.astype(jnp.bfloat16), EVERY, scatter_dimension=0, t...  457 us
    all_gather x4, waiting for transfers between devices, gather_matrix(): return lax.all_gather(own, EVERY, axis=0, tiled=True)  161 us
    all_gather x1, waiting for transfers between devices, reduce_vectors(): total = jnp.sum(lax.all_gather(packed, EVERY), axis=0)  42.1 us
    all_gather x1, blocking collectives, gather_vectors(): whole = lax.all_gather(packed, 'dp', axis=0, tiled=False)  32.7 us
    dot_general x1, matrix products, forward_pass(): jnp.dot(hidden_in, w_up, preferred_element_type=jnp.float32)  26.8 us
    all_gather x2, waiting for transfers between devices, reduce_matrix(): return lax.all_gather(part, 'rep', axis=0, tiled=True).astype(jnp.float32)  22.6 us
  transfers between devices with their start and end apart: 11, of which 11 were waited for; matrix products, arithmetic and copies ran while one was open for 20% of the time, Pallas kernels for 0%

profile of v1, /device:TPU:0, one launch (start us, length us, event | category | flops | bytes accessed | tf_op | source)
XLA Modules:
  0.0 972.7 jit_solution(1005191101161576677)
XLA Ops:
  7.2 1.7 constant_dynamic-slice_fusion.4
  9.0 1.5 constant_dynamic-slice_fusion.3
  11.4 1.7 constant_dynamic-slice_fusion.1
  13.8 0.9 dynamic-update-slice.9
  14.7 0.8 dynamic-update-slice.10
  15.5 0.8 dynamic-update-slice.11
  16.3 0.9 dynamic-update-slice.12
  17.2 0.8 dynamic-update-slice.13
  18.0 0.8 dynamic-update-slice.14
  18.9 0.8 dynamic-update-slice.15
  19.7 0.8 dynamic-update-slice.16
  20.5 0.8 dynamic-update-slice.17
  21.3 32.7 %all-gather.2 = bf16[8,1,1536]{2,1,0:T(2,128)(2,1)S(1)} all-gather(bf16[1,1,1536]{2,1,0:T(2,128)(2,1)S(1)} %reshape.395), channel_id=2, replica_groups=mesh['dp'=8,'rep'=4] {'dp'}, dimensions={0}, use_global_device_ids=true | all-gather | bytes 27648 | tf_op jit(solution)/shard_map/all_gather | solution.py:303
  54.1 3.7 fusion.47
  58.0 2.6 copy.71
  60.6 3.7 reshape.368
  64.3 1.9 copy.72
  67.8 1.5 fusion.30
  69.3 14.1 %all-gather.11.cloned.1.call-done = bf16[1024,3072]{1,0:T(8,128)(2,1)} async-done(((bf16[32,3072]{1,0:T(8,128)(2,1)}), bf16[1024,3072]{1,0:T(8,128)(2,1)}) %all-gather.11.cloned.1.call-update) | async-done | bytes 6291472 | tf_op jit(solution)/shard_map/all_gather | solution.py:298
  83.4 5.8 fusion.65
  89.2 1.1 slice.165
  90.4 1.6 fusion.39
  92.5 1.9 copy.75
  94.4 2.7 copy.73
  97.1 7.4 fusion.63
  104.4 8.4 fusion
  112.9 8.7 fusion.41
  121.5 19.5 %all-gather.13.cloned.1.call-done = bf16[1024,1024]{1,0:T(8,128)(2,1)} async-done(((bf16[32,1024]{1,0:T(8,128)(2,1)}), bf16[1024,1024]{1,0:T(8,128)(2,1)}) %all-gather.13.cloned.1.call-update) | async-done | bytes 2097168 | tf_op jit(solution)/shard_map/all_gather | solution.py:298
  141.1 3.3 fusion.64
  144.7 75.7 %all-gather.15.cloned.1.call-done = bf16[1024,4096]{1,0:T(8,128)(2,1)} async-done(((bf16[32,4096]{1,0:T(8,128)(2,1)}), bf16[1024,4096]{1,0:T(8,128)(2,1)}) %all-gather.15.cloned.1.call-update) | async-done | bytes 8388624 | tf_op jit(solution)/shard_map/all_gather | solution.py:298
  220.4 26.8 %fusion.4 = (bf16[512,4096]{1,0:T(8,128)(2,1)}, f32[512,4096]{1,0:T(8,128)}) fusion(f32[4096]{0:T(1024)S(1)} %bitcast.148, bf16[1024,4096]{1,0:T(8,128)(2,1)} %all-gather.15.cloned.1.call-done, f32[512,1024]{1,0:T(8,128)S(1)} %get-tuple-element.106, f32[1024]{0:T(1024)S(1)} %get-tuple-element.94, f32[1024]{0:T(1024)S(1)} %get-tuple-element.95, ...), kind=kOutput, calls=%fused_computation.12 | convolution fusion | flops 4436000768 | bytes 23097344 | tf_op jit(solution)/shard_map/dot_general | solution.py:172
  247.3 51.6 %all-gather.17.cloned.1.call-done = bf16[4096,1024]{1,0:T(8,128)(2,1)} async-done(((bf16[128,1024]{1,0:T(8,128)(2,1)}), bf16[4096,1024]{1,0:T(8,128)(2,1)}) %all-gather.17.cloned.1.call-update) | async-done | bytes 8388624 | tf_op jit(solution)/shard_map/all_gather | solution.py:298
  298.8 12.1 %convert_reduce_fusion = (f32[4096]{0:T(1024)S(1)}, bf16[512,4096]{1,0:T(8,128)(2,1)S(1)}) fusion(f32[512,4096]{1,0:T(8,128)} %get-tuple-element.108, f32[4096]{0:T(1024)S(1)} %bitcast.149, bf16[4096,1024]{1,0:T(8,128)(2,1)} %all-gather.17.cloned.1.call-done, bf16[512,1024]{1,0:T(8,128)(2,1)} %param.18), kind=kOutput, calls=%fused_computation.20 | convolution fusion | flops 4322226176 | bytes 22052864 | tf_op jit(solution)/shard_map/td,fd->tf/dot_general | solution.py:234
  311.0 2.1 copy-done.35
  313.1 7.5 convolution_convert_fusion.1
  320.7 10.3 %convolution_convert_fusion = bf16[4096,1024]{1,0:T(8,128)(2,1)} fusion(bf16[512,4096]{1,0:T(8,128)(2,1)} %get-tuple-element.107, bf16[512,1024]{1,0:T(8,128)(2,1)} %param.18), kind=kOutput, calls=%fused_computation.38 | convolution fusion | flops 4299161600 | bytes 13631488 | tf_op jit(solution)/shard_map/tf,td->fd/dot_general | solution.py:232
  331.7 9.8 %multiply_reduce_fusion.1 = (f32[1024]{0:T(1024)}, f32[512]{0:T(512)S(1)}, f32[512]{0:T(512)S(1)}, f32[1024]{0:T(1024)}, f32[512,1024]{1,0:T(8,128)S(1)}) fusion(f32[512,1024]{1,0:T(8,128)S(1)} %get-tuple-element.106, f32[512]{0:T(512)S(1)} %add_rsqrt_fusion, f32[512]{0:T(512)S(1)} %broadcast_multiply_fusion.4, f32[1024]{0:T(1024)S(1)} %get-tuple-element.95, ...), kind=kOutput, calls=%fused_computation.70 | convolution fusion | flops 4299682816 | bytes 16797696 | tf_op jit(solution)/shard_map/tf,df->td/dot_general | solution.py:238
  341.4 0.9 convert_reduce_fusion.3
  342.4 1.3 copy-done.12
  343.7 1.3 convolution_convert_fusion.4
  345.6 9.9 %convert_reduce_fusion.4 = (f32[16,64]{1,0:T(8,128)S(1)}, bf16[16,64,512]{2,1,0:T(8,128)(2,1)}) fusion(bf16[512,16,64]{0,2,1:T(8,128)(2,1)S(1)} %bitcast.134, f32[16,512,512]{1,2,0:T(8,128)} %get-tuple-element.104, f32[16,512]{1,0:T(8,128)S(1)} %log_add_fusion), kind=kOutput, calls=%fused_computation.72 | convolution fusion | flops 546831360 | bytes 18911232 | tf_op jit(solution)/shard_map/while/body/eval_jaxpr/hqk,qhd->khd/dot_general | solution.py:86
  355.5 10.6 %multiply_reduce_fusion = (f32[16,512]{1,0:T(8,128)}, f32[16,512,512]{1,2,0:T(8,128)S(1)}) fusion(f32[16,512,512]{1,2,0:T(8,128)} %get-tuple-element.104, f32[16,512]{1,0:T(8,128)} %copy-done.22, bf16[512,16,64]{0,2,1:T(8,128)(2,1)} %bitcast.135, bf16[512,16,64]{0,2,1:T(8,128)(2,1)} %bitcast.136), kind=kOutput, calls=%fused_computation.1 | convolution fusion | flops 549445632 | bytes 35717120 | tf_op jit(solution)/shard_map/while/body/eval_jaxpr/qhd,khd->hqk/dot_general | solution.py:92
  366.1 8.3 multiply_convert_fusion
  374.5 2.9 convert_reduce_fusion.5
  378.1 6.2 multiply_convert_fusion.1
  384.4 8.9 fusion.36
  394.1 3.8 convolution_convert_fusion.3
  398.0 8.1 convolution_convert_fusion.2
  406.2 63.3 %reduce-scatter.9.cloned.1.call-done = bf16[32,4096]{1,0:T(8,128)(2,1)} async-done(((bf16[1024,4096]{1,0:T(8,128)(2,1)}), bf16[32,4096]{1,0:T(8,128)(2,1)}) %reduce-scatter.9.cloned.1.call-update) | async-done | bytes 262160 | tf_op jit(solution)/shard_map/reduce_scatter | solution.py:312
  469.8 147.7 %reduce-scatter.11.cloned.1.call-done = bf16[128,1024]{1,0:T(8,128)(2,1)} async-done(((bf16[4096,1024]{1,0:T(8,128)(2,1)}), bf16[128,1024]{1,0:T(8,128)(2,1)}) %reduce-scatter.11.cloned.1.call-update) | async-done | bytes 262160 | tf_op jit(solution)/shard_map/reduce_scatter | solution.py:312
  617.6 10.3 %add_convert_fusion = bf16[512,1024]{1,0:T(8,128)(2,1)} fusion(f32[512,1024]{1,0:T(8,128)S(1)} %copy-done.6, bf16[512,4096]{1,0:T(8,128)(2,1)} %get-tuple-element.107, bf16[4096,1024]{1,0:T(8,128)(2,1)} %all-gather.17.cloned.1.call-done, f32[1024]{0:T(1024)S(1)} %copy-done.32), kind=kOutput, calls=%fused_computation.77 | convolution fusion | flops 4296540160 | bytes 15732736 | tf_op jit(solution)/shard_map/dot_general | solution.py:178
  627.9 1.7 fusion.35
  629.7 42.1 %all-gather.23.cloned.1.call-done = f32[256,1536]{1,0:T(8,128)} async-done(((f32[8,1536]{1,0:T(8,128)}), f32[256,1536]{1,0:T(8,128)}) %all-gather.23.cloned.1.call-update) | async-done | bytes 1572880 | tf_op jit(solution)/shard_map/all_gather | solution.py:319
  671.7 1.5 bitcast_reduce_fusion
  674.5 136.7 %reduce-scatter.7.cloned.1.call-done = bf16[32,1024]{1,0:T(8,128)(2,1)} async-done(((bf16[1024,1024]{1,0:T(8,128)(2,1)}), bf16[32,1024]{1,0:T(8,128)(2,1)}) %reduce-scatter.7.cloned.1.call-update) | async-done | bytes 65552 | tf_op jit(solution)/shard_map/reduce_scatter | solution.py:312
  811.2 6.0 all_gather.45
  817.2 0.8 convert_element_type.253
  818.0 109.7 %reduce-scatter.5.cloned.1.call-done = bf16[32,3072]{1,0:T(8,128)(2,1)} async-done(((bf16[1024,3072]{1,0:T(8,128)(2,1)}), bf16[32,3072]{1,0:T(8,128)(2,1)}) %reduce-scatter.5.cloned.1.call-update) | async-done | bytes 196624 | tf_op jit(solution)/shard_map/reduce_scatter | solution.py:312
  927.7 8.8 all_gather.42
  936.5 1.3 convert_element_type.247
  937.8 7.0 all-gather.19.cloned.1.call-done
  944.8 2.8 convert_element_type.255
  947.6 15.5 %all-gather.21.cloned.1.call-done = bf16[512,1024]{1,0:T(8,128)(2,1)} async-done(((bf16[128,1024]{1,0:T(8,128)(2,1)}), bf16[512,1024]{1,0:T(8,128)(2,1)}) %all-gather.21.cloned.1.call-update) | async-done | bytes 1048592 | tf_op jit(solution)/shard_map/all_gather | solution.py:313
  963.1 2.8 convert_element_type.257
  (130 shorter events, 8.3 us)
Async XLA Ops:
  7.2 3.4 copy-start
  7.2 76.2 %all-gather.11.cloned.1.call-start = ((), (), s32[]{:S(2)}) async-start(), calls=%async_computation.4 | async-start | bytes 6488064 | tf_op jit(solution)/shard_map/all_gather | solution.py:298
  9.0 132.1 %all-gather.13.cloned.1.call-start = ((), (), s32[]{:S(2)}) async-start(), calls=%async_computation.5 | async-start | bytes 2162688 | tf_op jit(solution)/shard_map/all_gather | solution.py:298
  10.5 209.9 %all-gather.15.cloned.1.call-start = ((), (), s32[]{:S(2)}) async-start(), calls=%async_computation.6 | async-start | bytes 8650752 | tf_op jit(solution)/shard_map/all_gather | solution.py:298
  11.3 287.5 %all-gather.17.cloned.1.call-start = ((), (), s32[]{:S(2)}) async-start(), calls=%async_computation.7 | async-start | bytes 8650752 | tf_op jit(solution)/shard_map/all_gather | solution.py:298
  13.1 456.4 %reduce-scatter.9.cloned.1.call-start = ((), (), s32[]{:S(2)}) async-start(), calls=%async_computation.10 | async-start | bytes 8650752 | tf_op jit(solution)/shard_map/reduce_scatter | solution.py:312
  58.0 8.2 copy-start.3
  60.6 6.9 copy-start.31
  66.5 22.7 %copy-start.27 = (f32[512]{0:T(512)}, f32[512]{0:T(512)S(1)}, u32[]{:S(2)}) copy-start(f32[512]{0:T(512)S(1)} %broadcast_multiply_fusion.5) | copy-start | bytes 6148
  66.9 22.3 %copy-start.29 = (f32[512]{0:T(512)}, f32[512]{0:T(512)S(1)}, u32[]{:S(2)}) copy-start(f32[512]{0:T(512)S(1)} %add_rsqrt_fusion.1) | copy-start | bytes 6148
  67.5 21.7 %copy-start.25 = (f32[1024]{0:T(1024)}, f32[1024]{0:T(1024)S(1)}, u32[]{:S(2)}) copy-start(f32[1024]{0:T(1024)S(1)} %get-tuple-element.100) | copy-start | bytes 12292
  92.5 12.0 %copy-start.9 = (bf16[512,1024]{0,1:T(8,128)(2,1)}, bf16[512,1024]{0,1:T(8,128)(2,1)S(1)}, u32[]{:S(2)}) copy-start(bf16[512,1024]{0,1:T(8,128)(2,1)S(1)} %copy.74) | copy-start | bytes 3145732
  94.4 10.1 %copy-start.7 = (bf16[512,1024]{0,1:T(8,128)(2,1)}, bf16[512,1024]{0,1:T(8,128)(2,1)S(1)}, u32[]{:S(2)}) copy-start(bf16[512,1024]{0,1:T(8,128)(2,1)S(1)} %copy.75) | copy-start | bytes 3145732
  104.4 8.4 copy-start.15
  144.3 197.1 %copy-start.5 = (f32[512,1024]{1,0:T(8,128)}, f32[512,1024]{1,0:T(8,128)S(1)}, u32[]{:S(2)}) copy-start(f32[512,1024]{1,0:T(8,128)S(1)} %get-tuple-element.106) | copy-start | bytes 6291460
  311.0 2.1 copy-start.35
  320.6 296.9 %reduce-scatter.11.cloned.1.call-start = ((), (), s32[]{:S(2)}) async-start(), calls=%async_computation.12 | async-start | bytes 8650752 | tf_op jit(solution)/shard_map/reduce_scatter | solution.py:312
  331.0 340.8 %all-gather.23.cloned.1.call-start = ((), (), s32[]{:S(2)}) async-start(), calls=%async_computation.14 | async-start | bytes 1622016 | tf_op jit(solution)/shard_map/all_gather | solution.py:319
  331.0 14.5 %copy-start.22 = (f32[16,512]{1,0:T(8,128)}, f32[16,512]{1,0:T(8,128)S(1)}, u32[]{:S(2)}) copy-start(f32[16,512]{1,0:T(8,128)S(1)} %log_add_fusion) | copy-start | bytes 98308
  331.7 9.8 %copy-start.20 = (bf16[512,1024]{1,0:T(8,128)(2,1)S(1)}, bf16[512,1024]{1,0:T(8,128)(2,1)}, u32[]{:S(2)}) copy-start(bf16[512,1024]{1,0:T(8,128)(2,1)} %param.18) | copy-start | bytes 3145732
  341.4 2.3 copy-start.18
  342.3 1.3 copy-start.12
  345.5 9.9 %copy-start.11 = (bf16[512,1024]{0,1:T(8,128)(2,1)}, bf16[512,1024]{0,1:T(8,128)(2,1)S(1)}, u32[]{:S(2)}) copy-start(bf16[512,1024]{0,1:T(8,128)(2,1)S(1)} %copy.77) | copy-start | bytes 3145732
  366.1 8.3 copy-start.8
  374.4 3.6 copy-start.2
  374.4 3.6 copy-start.23
  374.5 3.7 copy-start.10
  378.0 6.4 copy-start.26
  378.0 6.4 copy-start.28
  378.0 6.4 copy-start.30
  378.1 6.3 copy-start.16
  384.3 9.0 copy-start.21
  384.4 9.0 copy-start.34
  384.4 9.0 copy-start.33
  384.4 9.7 copy-start.13
  393.4 0.6 copy-start.24
  393.4 4.6 copy-start.17
  394.1 417.1 %reduce-scatter.7.cloned.1.call-start = ((), (), s32[]{:S(2)}) async-start(), calls=%async_computation.9 | async-start | bytes 2162688 | tf_op jit(solution)/shard_map/reduce_scatter | solution.py:312
  398.0 529.7 %reduce-scatter.5.cloned.1.call-start = ((), (), s32[]{:S(2)}) async-start(), calls=%async_computation.8 | async-start | bytes 6488064 | tf_op jit(solution)/shard_map/reduce_scatter | solution.py:312
  406.1 211.5 %copy-start.6 = (f32[512,1024]{1,0:T(8,128)S(1)}, f32[512,1024]{1,0:T(8,128)}, u32[]{:S(2)}) copy-start(f32[512,1024]{1,0:T(8,128)} %copy-done.5) | copy-start | bytes 6291460
  406.1 211.5 %copy-start.32 = (f32[1024]{0:T(1024)S(1)}, f32[1024]{0:T(1024)}, u32[]{:S(2)}) copy-start(f32[1024]{0:T(1024)} %get-tuple-element.93) | copy-start | bytes 12292
  406.1 538.7 %all-gather.19.cloned.1.call-start = ((), (), s32[]{:S(2)}) async-start(), calls=%async_computation.11 | async-start | bytes 1310720 | tf_op jit(solution)/shard_map/all_gather | solution.py:313
  469.5 493.6 %all-gather.21.cloned.1.call-start = ((), (), s32[]{:S(2)}) async-start(), calls=%async_computation.13 | async-start | bytes 1310720 | tf_op jit(solution)/shard_map/all_gather | solution.py:313
  617.6 10.3 %copy-start.4 = (bf16[512,1024]{1,0:T(8,128)(2,1)S(1)}, bf16[512,1024]{1,0:T(8,128)(2,1)}, u32[]{:S(2)}) copy-start(bf16[512,1024]{1,0:T(8,128)(2,1)} %param.17) | copy-start | bytes 3145732
  617.6 10.3 %copy-start.14 = (f32[512,1024]{1,0:T(8,128)S(1)}, f32[512,1024]{1,0:T(8,128)}, u32[]{:S(2)}) copy-start(f32[512,1024]{1,0:T(8,128)} %copy-done.12) | copy-start | bytes 6291460
  617.6 10.3 %copy-start.19 = (f32[512,1024]{1,0:T(8,128)S(1)}, f32[512,1024]{1,0:T(8,128)}, u32[]{:S(2)}) copy-start(f32[512,1024]{1,0:T(8,128)} %get-tuple-element.112) | copy-start | bytes 6291460
  627.9 338.0 %copy-start.1 = (bf16[128,4096]{1,0:T(8,128)(2,1)S(1)}, bf16[128,4096]{1,0:T(8,128)(2,1)}, u32[]{:S(2)}) copy-start(bf16[128,4096]{1,0:T(8,128)(2,1)} %param.26) | copy-start | bytes 3145732
Sparse Core Ops, SparseCore 0:
  11.4 71.9 all-gather.10
  86.3 54.7 all-gather.12
  144.5 75.8 all-gather.14
  223.1 75.6 all-gather.16
  320.8 148.6 reduce-scatter.8
  471.6 145.8 reduce-scatter.10
  621.0 50.6 all-gather.22
  674.0 137.1 reduce-scatter.6
  816.8 110.8 reduce-scatter.4
  929.1 15.6 all-gather.18
  946.4 16.6 all-gather.20
